TPU v7x, 128 devices: a whole 4x4x4 slice. The times are simulated.
128 devices in a mesh: brick: 64 (over z_lo, x, y, core), vec: 2 (over z_hi).
Axes of the slice: x: 4, y: 4, z: 4 (z_hi: 2, z_lo: 2; z = z_hi * 2 + z_lo), core: 2. Of those that a mesh axis runs over, the one named last changes fastest.
Arguments:
- levels: int32 [12, 2048, 16, 128], P(None, 'brick'), may hold values from 0 to 255
- start_block: int32 [16, 2048, 16, 128], P('vec', 'brick'), may hold values from -8 to 8
Outputs:
- alpha_blocks: float32 [1, 16, 16], replicated
- beta_blocks: float32 [1, 16, 16], replicated
- basis: float32 [16, 2048, 16, 128], P('vec', 'brick')
All inputs are finite; a program needn't handle non-finite values.
Results may differ from a plain program's by a relative error of at most 0.00026.
Values sent between devices are 32-bit elements; how exact they have to be, the bound alone decides.
No kernel may reach another device: no remote copies, remote signals or barrier semaphores. Data moves between devices by JAX's collectives and lax.ppermute only.
A program may use at most 128 MiB of HBM per device.

v0:
```python
import math
import jax
import jax.numpy as jnp
from jax import lax
from jax.sharding import PartitionSpec as P

offsets_cube = (1, 3, 9, 27)
deepest = 27
highest = lax.Precision.HIGHEST


def passed_along(value, axis, by):
    size = lax.axis_size(axis)
    pairs = [(i, i + by) for i in range(size) if 0 <= i + by < size]
    return lax.ppermute(value, axis, pairs)


def forward_take(field_in, offset, axis_dim):
    length_dim = field_in.shape[axis_dim]
    widths = [(0, 0)] * field_in.ndim
    widths[axis_dim] = (0, offset)
    return lax.slice_in_dim(jnp.pad(field_in, widths), offset, offset + length_dim, axis=axis_dim)


def backward_put(field_in, offset, axis_dim):
    length_dim = field_in.shape[axis_dim]
    widths = [(0, 0)] * field_in.ndim
    widths[axis_dim] = (offset, 0)
    return lax.slice_in_dim(jnp.pad(field_in, widths), 0, length_dim, axis=axis_dim)


def local_planes(field_in, weights, result):
    for axis_dim in (2, 3):
        for position, offset in enumerate(offsets_cube):
            channel = weights[4 * (axis_dim - 1) + position]
            result = (
                result
                + channel * forward_take(field_in, offset, axis_dim)
                + backward_put(channel * field_in, offset, axis_dim)
            )
    return result


def apply_carried(field_in, weights):
    row_count = field_in.shape[1]
    upper_rows = passed_along(field_in[:, :deepest], "brick", -1)
    extended = jnp.concatenate([field_in, upper_rows], axis=1)
    result = jnp.zeros_like(field_in)
    spilled = jnp.zeros_like(upper_rows)
    for position, offset in enumerate(offsets_cube):
        channel = weights[position]
        result = result + channel * extended[:, offset : offset + row_count]
        shifted_rows = jnp.pad(
            channel * field_in, ((0, 0), (offset, deepest - offset), (0, 0), (0, 0))
        )
        result = result + shifted_rows[:, :row_count]
        spilled = spilled + shifted_rows[:, row_count:]
    result = local_planes(field_in, weights, result)
    arrived = passed_along(spilled, "brick", 1)
    return result + jnp.pad(arrived, ((0, 0), (0, row_count - deepest), (0, 0), (0, 0)))


def inner_of(left_rows, right_rows):
    return jnp.einsum("in,jn->ij", left_rows, right_rows, precision=highest)


def body(levels, start_block):
    weights = (levels.astype(jnp.float32) + 0.5) / 256.0

    def affinity_apply(field_in):
        return apply_carried(field_in, weights)

    unit_field = jnp.ones((1,) + levels.shape[1:], jnp.float32)
    degree = affinity_apply(unit_field)[0] + 1.0
    inv_root = lax.rsqrt(degree)

    def half_step(block_in):
        return 0.5 * (block_in + inv_root * affinity_apply(inv_root * block_in))

    own_cols = start_block.shape[0]
    grid_shape = start_block.shape
    voxel_total = lax.axis_size("brick") * grid_shape[1] * grid_shape[2] * grid_shape[3]

    def to_work(block_in):
        flat_block = block_in.reshape(own_cols, -1)
        work_rows = lax.all_gather(flat_block, "vec", axis=0, tiled=True)
        return work_rows

    def from_work(work_rows):
        own_rows = lax.dynamic_slice_in_dim(
            work_rows, lax.axis_index("vec") * own_cols, own_cols, 0
        )
        return own_rows.reshape(grid_shape)

    def total_one(partial_sum):
        summed = lax.psum(partial_sum, "brick")
        return summed

    start_work = to_work(start_block.astype(jnp.float32))
    lower_factor = jnp.linalg.cholesky(total_one(inner_of(start_work, start_work)))
    current = lax.linalg.triangular_solve(lower_factor, start_work, left_side=True, lower=True)
    basis_now = from_work(current)
    image_block = to_work(half_step(half_step(basis_now)))
    coeffs = total_one(inner_of(image_block, current))
    residual = image_block - jnp.einsum("ij,jn->in", coeffs, current, precision=highest)
    gram_matrix = total_one(inner_of(residual, residual))
    lower_factor = jnp.linalg.cholesky(gram_matrix)
    following = lax.linalg.triangular_solve(lower_factor, residual, left_side=True, lower=True)
    alpha_list = [coeffs]
    beta_list = [lower_factor]
    basis_now = from_work(following)
    basis = basis_now * math.sqrt(voxel_total)
    return (jnp.stack(alpha_list), jnp.stack(beta_list), basis)


def solution(mesh):
    return jax.shard_map(
        body,
        mesh=mesh,
        in_specs=(P(None, "brick", None, None), P("vec", "brick", None, None)),
        out_specs=(P(), P(), P("vec", "brick", None, None)),
        check_vma=False,
    )
```

profile of v0, /device:TPU:1, one launch (start us, length us, event | category | flops | bytes accessed | tf_op | source)
XLA Modules:
  0.0 726.9 jit_solution(13446341821634345445)
XLA Ops:
  7.2 1.7 convert_element_type.111
  9.0 2.5 copy.14
  11.6 0.7 slice.322
  12.3 3.3 collective-permute-start
  15.6 2.3 add_multiply_fusion
  17.9 0.8 fusion.126
  18.7 0.7 copy-done.23
  19.4 0.7 fusion.117
  20.1 3.2 collective-permute-start.1
  23.4 1.6 slice_bitcast_fusion.5
  24.9 1.5 collective-permute-done.1
  26.5 2.7 broadcast_multiply_fusion.24
  29.2 48.8 %all-gather.3.cloned.1.call-done = f32[16,65536]{1,0:T(8,128)} async-done(((f32[8,65536]{1,0:T(8,128)}), f32[16,65536]{1,0:T(8,128)}) %all-gather.3.cloned.1.call-update) | async-done | bytes 4194320 | tf_op jit(solution)/shard_map/all_gather | solution.py:86
  78.0 9.0 %fusion.127 = f32[16,16]{0,1:T(8,128)S(1)} fusion(f32[16,65536]{1,0:T(8,128)} %all-gather.3.cloned.1.call-done), kind=kOutput, calls=%fused_computation.264 | convolution fusion | flops 201326592 | bytes 4195328 | tf_op jit(solution)/shard_map/in,jn->ij/dot_general | solution.py:64
  87.0 140.6 %psum.21 = f32[16,16]{0,1:T(8,128)S(1)} all-reduce(f32[16,16]{0,1:T(8,128)S(1)} %fusion.127), channel_id=1, replica_groups=mesh['brick'=64,'vec'=2] {'brick'}, use_global_device_ids=true, to_apply=%region_0.1 | all-reduce | flops 256 | bytes 2048 | tf_op jit(solution)/shard_map/psum | solution.py:96
  227.6 0.1 copy.6
  227.7 1.5 cholesky.44
  229.2 0.6 compare_reduce_fusion.1
  229.8 0.6 fusion.118
  230.5 1.2 custom-call.6
  231.7 5.4 fusion.122
  237.1 0.1 constant_dynamic-slice_fusion
  237.3 1.8 copy-done.1
  239.1 2.1 broadcast_multiply_fusion.14
  241.2 0.1 slice.428
  241.4 4.7 collective-permute-start.2
  246.1 5.1 broadcast_multiply_fusion.12
  251.2 0.2 fusion.76
  251.4 1.2 copy-done.3
  252.6 2.1 collective-permute-start.3
  254.7 10.7 %collective-permute-done.2 = f32[8,27,16,128]{3,0,2,1:T(8,128)S(1)} collective-permute-done((f32[8,27,16,128]{3,0,2,1:T(8,128)S(1)}, f32[8,27,16,128]{3,0,2,1:T(8,128)S(1)}, u32[]{:S(2)}, u32[]{:S(2)}) %collective-permute-start.2) | collective-permute-done | bytes 1769504 | tf_op jit(solution)/shard_map/ppermute | solution.py:15
  265.3 8.6 %collective-permute-done.3 = f32[8,27,16,128]{3,0,2,1:T(8,128)S(1)} collective-permute-done((f32[8,27,16,128]{3,0,2,1:T(8,128)S(1)}, f32[8,27,16,128]{3,0,2,1:T(8,128)S(1)}, u32[]{:S(2)}, u32[]{:S(2)}) %collective-permute-start.3) | collective-permute-done | bytes 1769504 | tf_op jit(solution)/shard_map/ppermute | solution.py:15
  273.9 1.2 copy-done.32
  275.2 12.9 %broadcast_multiply_fusion.13 = (f32[8,32,16,128]{3,0,2,1:T(8,128)}, f32[8,32,16,128]{3,0,2,1:T(8,128)S(1)}, f32[8,32,16,128]{3,0,2,1:T(8,128)}) fusion(f32[32,16,128]{2,1,0:T(8,128)} %get-tuple-element.20, f32[32,16,128]{2,1,0:T(8,128)} %get-tuple-element.11, f32[8,32,16,128]{3,0,2,1:T(8,128)} %bitcast.67, f32[8,27,16,128]{3,0,2,1:T(8,128)} %copy-done.32, ...), kind=kLoop, calls=%fused_computation.155 | loop fusion | flops 22020096 | bytes 40763392 | tf_op jit(solution)/shard_map/mul | solution.py:39
  288.2 0.1 slice.436
  288.3 0.8 copy-done.8
  289.1 0.1 copy-done.10
  289.2 0.1 copy-done.12
  289.2 0.1 copy-done.14
  289.3 0.1 copy-done.16
  289.4 0.1 copy-done.18
  289.5 0.1 copy-done.20
  289.6 5.1 broadcast_multiply_fusion.11
  294.7 1.9 collective-permute-start.4
  296.6 0.2 fusion.79
  296.8 4.5 collective-permute-start.5
  301.3 17.9 %collective-permute-done.4 = f32[8,27,16,128]{3,0,2,1:T(8,128)S(1)} collective-permute-done((f32[8,27,16,128]{3,0,2,1:T(8,128)S(1)}, f32[8,27,16,128]{3,0,2,1:T(8,128)S(1)}, u32[]{:S(2)}, u32[]{:S(2)}) %collective-permute-start.4) | collective-permute-done | bytes 1769504 | tf_op jit(solution)/shard_map/ppermute | solution.py:15
  319.2 1.5 collective-permute-done.5
  320.8 1.2 copy-done.30
  322.0 11.3 %add_multiply_fusion.1 = f32[8,32,16,128]{3,0,2,1:T(8,128)} fusion(f32[8,32,16,128]{3,0,2,1:T(8,128)} %get-tuple-element.10, f32[8,27,16,128]{3,0,2,1:T(8,128)} %copy-done.30, f32[8,32,16,128]{3,0,2,1:T(8,128)} %get-tuple-element.40, f32[8,32,16,128]{3,0,2,1:T(8,128)S(1)} %get-tuple-element.9, f32[8,32,16,128]{3,0,2,1:T(8,128)} %get-tuple-element.47, ...), kind=kLoop, calls=%fused_computation.134 | loop fusion | flops 22020096 | bytes 36306944 | tf_op jit(solution)/shard_map/mul | solution.py:78
  333.3 65.7 %all-gather.5.cloned.1.call-done = f32[16,65536]{1,0:T(8,128)} async-done(((f32[8,65536]{1,0:T(8,128)}), f32[16,65536]{1,0:T(8,128)}) %all-gather.5.cloned.1.call-update) | async-done | bytes 4194320 | tf_op jit(solution)/shard_map/all_gather | solution.py:86
  399.0 8.7 %fusion.128 = f32[16,16]{1,0:T(8,128)S(1)} fusion(f32[16,65536]{1,0:T(8,128)} %all-gather.5.cloned.1.call-done, f32[16,65536]{1,0:T(8,128)} %copy-done.1), kind=kOutput, calls=%fused_computation.265 | convolution fusion | flops 201326592 | bytes 8389632 | tf_op jit(solution)/shard_map/in,jn->ij/dot_general | solution.py:64
  407.7 140.9 %psum.22 = f32[16,16]{1,0:T(8,128)S(1)} all-reduce(f32[16,16]{1,0:T(8,128)S(1)} %fusion.128), channel_id=1, replica_groups=mesh['brick'=64,'vec'=2] {'brick'}, use_global_device_ids=true, to_apply=%region_3.6 | all-reduce | flops 256 | bytes 2048 | tf_op jit(solution)/shard_map/psum | solution.py:96
  548.6 7.1 convolution_subtract_fusion
  555.7 1.9 copy-done
  557.7 5.6 fusion.129
  563.3 144.8 %psum.23 = f32[16,16]{0,1:T(8,128)S(1)} all-reduce(f32[16,16]{0,1:T(8,128)S(1)} %fusion.129), channel_id=1, replica_groups=mesh['brick'=64,'vec'=2] {'brick'}, use_global_device_ids=true, to_apply=%region_4.7 | all-reduce | flops 256 | bytes 2048 | tf_op jit(solution)/shard_map/psum | solution.py:96
  708.2 1.5 cholesky.55
  709.7 0.6 compare_reduce_fusion
  710.4 1.2 select_bitcast_fusion
  711.6 1.2 custom-call.7
  712.8 5.4 fusion.119
  718.3 0.1 dynamic-slice_multiply_fusion
  718.4 1.7 copy.9
  (68 shorter events, 0.4 us)
Async XLA Ops:
  7.2 70.8 %all-gather.3.cloned.1.call-start = ((), (), s32[]{:S(2)}) async-start(), calls=%async_computation | async-start | bytes 6291456 | tf_op jit(solution)/shard_map/all_gather | solution.py:86
  11.5 387.5 %all-gather.5.cloned.1.call-start = ((), (), s32[]{:S(2)}) async-start(), calls=%async_computation.1 | async-start | bytes 6291456 | tf_op jit(solution)/shard_map/all_gather | solution.py:86
  12.3 12.7 %collective-permute-start = (f32[1,27,16,128]{3,2,1,0:T(8,128)}, f32[1,27,16,128]{3,2,1,0:T(8,128)}, u32[]{:S(2)}, u32[]{:S(2)}) collective-permute-start(f32[1,27,16,128]{3,2,1,0:T(8,128)} %slice.322), channel_id=1, source_target_pairs={{2,0},{4,2},{6,4},{8,6},{10,8},{12,10},{14,12},{16,14},{18,16},{20... | collective-permute-start | bytes 663560 | tf_op jit(solution)/shard_map/ppermute | solution.py:15
  18.7 0.7 copy-start.23
  18.7 1.4 copy-start.25
  18.7 4.6 copy-start.27
  20.1 6.4 collective-permute-start.1
  23.3 3.2 copy-start.24
  23.3 3.2 copy-start.26
  23.3 3.2 copy-start.28
  23.3 3.2 copy-start.33
  237.1 2.0 copy-start.1
  237.1 2.0 copy-start.21
  237.1 1.9 copy-start.22
  239.1 2.1 copy-start.2
  241.2 4.9 copy-start.5
  241.2 4.9 copy-start.6
  241.2 4.9 copy-start.7
  241.2 4.9 copy-start.9
  241.2 4.9 copy-start.11
  241.2 4.9 copy-start.13
  241.2 4.9 copy-start.15
  241.2 4.9 copy-start.17
  241.2 4.9 copy-start.19
  241.4 24.0 %collective-permute-start.2 = (f32[8,27,16,128]{3,0,2,1:T(8,128)S(1)}, f32[8,27,16,128]{3,0,2,1:T(8,128)S(1)}, u32[]{:S(2)}, u32[]{:S(2)}) collective-permute-start(f32[8,27,16,128]{3,0,2,1:T(8,128)S(1)} %slice.428), channel_id=1, source_target_pairs={{2,0},{4,2},{6,4},{8,6},{10,8},{12,10},{14,12},{16,14},{18,16},{20... | collective-permute-start | bytes 5308424 | tf_op jit(solution)/shard_map/ppermute | solution.py:15
  251.2 1.4 copy-start.3
  252.6 21.4 %collective-permute-start.3 = (f32[8,27,16,128]{3,0,2,1:T(8,128)S(1)}, f32[8,27,16,128]{3,0,2,1:T(8,128)S(1)}, u32[]{:S(2)}, u32[]{:S(2)}) collective-permute-start(f32[8,27,16,128]{3,0,2,1:T(8,128)S(1)} %fusion.76), channel_id=1, source_target_pairs={{0,2},{2,4},{4,6},{6,8},{8,10},{10,12},{12,14},{14,16},{16,18},{18... | collective-permute-start | bytes 5308424 | tf_op jit(solution)/shard_map/ppermute | solution.py:15
  265.3 8.6 %copy-start.31 = (f32[8,27,16,128]{3,0,2,1:T(8,128)}, f32[8,27,16,128]{3,0,2,1:T(8,128)S(1)}, u32[]{:S(2)}) copy-start(f32[8,27,16,128]{3,0,2,1:T(8,128)S(1)} %collective-permute-done.2) | copy-start | bytes 5308420
  273.9 1.2 copy-start.32
  288.1 1.0 copy-start.8
  288.1 1.0 copy-start.10
  288.1 1.1 copy-start.12
  288.2 1.2 copy-start.14
  288.2 1.2 copy-start.16
  288.2 1.3 copy-start.18
  288.2 1.4 copy-start.20
  294.7 24.6 %collective-permute-start.4 = (f32[8,27,16,128]{3,0,2,1:T(8,128)S(1)}, f32[8,27,16,128]{3,0,2,1:T(8,128)S(1)}, u32[]{:S(2)}, u32[]{:S(2)}) collective-permute-start(f32[8,27,16,128]{3,0,2,1:T(8,128)S(1)} %slice.436), channel_id=1, source_target_pairs={{2,0},{4,2},{6,4},{8,6},{10,8},{12,10},{14,12},{16,14},{18,16},{20... | collective-permute-start | bytes 5308424 | tf_op jit(solution)/shard_map/ppermute | solution.py:15
  296.6 25.4 %copy-start.4 = (f32[8,32,16,128]{3,0,2,1:T(8,128)S(1)}, f32[8,32,16,128]{3,0,2,1:T(8,128)}, u32[]{:S(2)}) copy-start(f32[8,32,16,128]{3,0,2,1:T(8,128)} %get-tuple-element.8) | copy-start | bytes 6291460
  296.8 24.0 %collective-permute-start.5 = (f32[8,27,16,128]{3,0,2,1:T(8,128)S(1)}, f32[8,27,16,128]{3,0,2,1:T(8,128)S(1)}, u32[]{:S(2)}, u32[]{:S(2)}) collective-permute-start(f32[8,27,16,128]{3,0,2,1:T(8,128)S(1)} %fusion.79), channel_id=1, source_target_pairs={{0,2},{2,4},{4,6},{6,8},{8,10},{10,12},{12,14},{14,16},{16,18},{18... | collective-permute-start | bytes 5308424 | tf_op jit(solution)/shard_map/ppermute | solution.py:15
  319.2 1.5 copy-start.29
  320.7 1.2 copy-start.30
  548.6 7.1 copy-start.34
  555.7 2.0 copy-start
Sparse Core Ops, SparseCore 0:
  11.6 66.3 all-gather.2
  333.4 65.5 all-gather.4
where the time goes:
time: 727 us
  blocking collectives  426 us (59%)
  waiting for transfers between devices  155 us (21%)
  other arithmetic  54.6 us (8%)
  matrix products  41.2 us (6%)
  starting transfers between devices  19.7 us (3%)
  local copies, waits for them, and re-layouts  15.7 us (2%)
  between operations  14.6 us (2%)
    psum x3, blocking collectives, total_one(): summed = lax.psum(partial_sum, 'brick')  426 us
    all_gather x2, waiting for transfers between devices, to_work(): work_rows = lax.all_gather(flat_block, 'vec', axis=0, tiled=True)  115 us
    ppermute x6, waiting for transfers between devices, passed_along(): return lax.ppermute(value, axis, pairs)  40.2 us
    mul x4, other arithmetic, local_planes(): channel * field_in  25.2 us
    dot_general x3, matrix products, inner_of(): return jnp.einsum('in,jn->ij', left_rows, right_rows, precision=highest)  23.3 us
    ppermute x6, starting transfers between devices, passed_along(): return lax.ppermute(value, axis, pairs)  19.7 us
  transfers between devices with their start and end apart: 8, of which 7 were waited for; matrix products, arithmetic and copies ran while one was open for 2% of the time, Pallas kernels for 0%

commit v1 on v0

--- a/solution.py
+++ b/solution.py
@@ -83,7 +83,9 @@
 
     def to_work(block_in):
         flat_block = block_in.reshape(own_cols, -1)
-        work_rows = lax.all_gather(flat_block, "vec", axis=0, tiled=True)
+        work_rows = jnp.concatenate(
+            lax.all_to_all(jnp.stack([flat_block] * lax.axis_size("vec")), "vec", 0, 0), axis=0
+        )
         return work_rows
 
     def from_work(work_rows):

time: 727 us -> 696 us (0.957)
  waiting for transfers between devices: 155 us -> 75 us
  blocking collectives: 426 us -> 469 us
  between operations: 14.6 us -> 1.16 us
  starting transfers between devices: 19.7 us -> 27.7 us
  other arithmetic: 54.6 us -> 61.9 us
    all_gather x2 -> x0, waiting for transfers between devices: 115 us -> none  [to_work(): work_rows = lax.all_gather(flat_block, 'vec', axis=0, tiled=True)]
    all_to_all x0 -> x1, blocking collectives: none -> 36 us  [to_work(): lax.all_to_all(jnp.stack([flat_block] * lax.axis_size('vec')), 'vec', 0, 0)]
    all_to_all x0 -> x1, waiting for transfers between devices: none -> 34.9 us  [to_work(): lax.all_to_all(jnp.stack([flat_block] * lax.axis_size('vec')), 'vec', 0, 0)]
  transfers between devices with their start and end apart: 8 -> 7, of which waited for: 7 -> 6; matrix products, arithmetic and copies ran while one was open for 2% -> 2% of each run, Pallas kernels for 0% -> 0%
where the time goes in v1:
time: 696 us; the launch traced here: 690 us
  blocking collectives  469 us (67%)
  waiting for transfers between devices  75 us (11%)
  other arithmetic  61.9 us (9%)
  matrix products  39.4 us (6%)
  starting transfers between devices  27.7 us (4%)
  local copies, waits for them, and re-layouts  15.2 us (2%)
    psum x3, blocking collectives, total_one(): summed = lax.psum(partial_sum, 'brick')  433 us
    ppermute x6, waiting for transfers between devices, passed_along(): return lax.ppermute(value, axis, pairs)  40.2 us
    all_to_all x1, blocking collectives, to_work(): lax.all_to_all(jnp.stack([flat_block] * lax.axis_size('vec')), 'vec', 0, 0)  36 us
    all_to_all x1, waiting for transfers between devices, to_work(): lax.all_to_all(jnp.stack([flat_block] * lax.axis_size('vec')), 'vec', 0, 0)  34.9 us
    mul x4, other arithmetic, local_planes(): channel * field_in  25.8 us
    ppermute x6, starting transfers between devices, passed_along(): return lax.ppermute(value, axis, pairs)  22 us
    dot_general x3, matrix products, inner_of(): return jnp.einsum('in,jn->ij', left_rows, right_rows, precision=highest)  21.5 us
    mul x2, other arithmetic, half_step(): return 0.5 * (block_in + inv_root * affinity_apply(inv_root * block_in))  14.4 us
  transfers between devices with their start and end apart: 7, of which 6 were waited for; matrix products, arithmetic and copies ran while one was open for 2% of the time, Pallas kernels for 0%

profile of v1, /device:TPU:1, one launch (start us, length us, event | category | flops | bytes accessed | tf_op | source)
XLA Modules:
  0.0 689.7 jit_solution(351898135808151558)
XLA Ops:
  0.6 3.1 convert_element_type.111
  3.7 2.0 stack_reshape.8
  5.7 2.3 pad_maximum_fusion
  8.0 5.7 all-to-all-start
  13.7 0.7 slice.322
  14.4 3.2 collective-permute-start
  17.6 2.3 add_multiply_fusion
  19.9 0.8 fusion.131
  20.7 0.7 copy-done.25
  21.4 0.7 fusion.123
  22.1 3.2 collective-permute-start.1
  25.4 1.7 slice_bitcast_fusion.5
  27.1 1.4 collective-permute-done.1
  28.6 2.6 broadcast_multiply_fusion.24
  31.1 34.9 %all-to-all-done = f32[2,8,65536]{2,1,0:T(8,128)} async-done(((f32[2,8,65536]{2,1,0:T(8,128)}), f32[2,8,65536]{2,1,0:T(8,128)}, u32[]{:S(2)}, u32[]{:S(2)}) %all-to-all-start) | async-done | bytes 4194336 | tf_op jit(solution)/shard_map/all_to_all | solution.py:87
  66.0 9.0 %fusion.4 = f32[16,16]{0,1:T(8,128)S(1)} fusion(f32[2,8,65536]{2,1,0:T(8,128)} %all-to-all-done), kind=kOutput, calls=%fused_computation.31 | convolution fusion | flops 201326592 | bytes 4195328 | tf_op jit(solution)/shard_map/in,jn->ij/dot_general | solution.py:64
  75.0 141.2 %psum.21 = f32[16,16]{0,1:T(8,128)S(1)} all-reduce(f32[16,16]{0,1:T(8,128)S(1)} %fusion.4), channel_id=1, replica_groups=mesh['brick'=64,'vec'=2] {'brick'}, use_global_device_ids=true, to_apply=%region_0.1 | all-reduce | flops 256 | bytes 2048 | tf_op jit(solution)/shard_map/psum | solution.py:98
  216.2 1.5 cholesky.44
  217.7 0.6 compare_reduce_fusion.1
  218.4 0.6 fusion.124
  219.0 1.2 custom-call.6
  220.2 5.4 fusion.2
  225.7 0.1 constant_dynamic-slice_fusion
  225.9 0.9 copy-done.23
  226.8 0.3 copy-done.24
  227.1 2.0 broadcast_multiply_fusion.14
  229.1 0.1 slice.428
  229.3 7.2 %collective-permute-start.2 = (f32[8,27,16,128]{3,0,2,1:T(8,128)S(1)}, f32[8,27,16,128]{3,0,2,1:T(8,128)}, u32[]{:S(2)}, u32[]{:S(2)}) collective-permute-start(f32[8,27,16,128]{3,0,2,1:T(8,128)S(1)} %slice.428), channel_id=1, source_target_pairs={{2,0},{4,2},{6,4},{8,6},{10,8},{12,10},{14,12},{16,14},{18,16},{20... | collective-permute-start | bytes 5308424 | tf_op jit(solution)/shard_map/ppermute | solution.py:15
  236.6 5.0 broadcast_multiply_fusion.12
  241.6 0.2 fusion.82
  241.8 1.1 copy-done.3
  242.9 0.7 copy-done.6
  243.6 2.1 collective-permute-start.3
  245.7 7.6 %collective-permute-done.2 = f32[8,27,16,128]{3,0,2,1:T(8,128)} collective-permute-done((f32[8,27,16,128]{3,0,2,1:T(8,128)S(1)}, f32[8,27,16,128]{3,0,2,1:T(8,128)}, u32[]{:S(2)}, u32[]{:S(2)}) %collective-permute-start.2) | collective-permute-done | bytes 1769504 | tf_op jit(solution)/shard_map/ppermute | solution.py:15
  253.3 11.6 %collective-permute-done.3 = f32[8,27,16,128]{3,0,2,1:T(8,128)S(1)} collective-permute-done((f32[8,27,16,128]{3,0,2,1:T(8,128)S(1)}, f32[8,27,16,128]{3,0,2,1:T(8,128)S(1)}, u32[]{:S(2)}, u32[]{:S(2)}) %collective-permute-start.3) | collective-permute-done | bytes 1769504 | tf_op jit(solution)/shard_map/ppermute | solution.py:15
  265.0 1.2 copy-done.33
  266.2 13.7 %broadcast_multiply_fusion.13 = (f32[8,32,16,128]{3,0,2,1:T(8,128)}, f32[8,32,16,128]{3,0,2,1:T(8,128)S(1)}, f32[8,32,16,128]{3,0,2,1:T(8,128)}) fusion(f32[32,16,128]{2,1,0:T(8,128)} %get-tuple-element.20, f32[32,16,128]{2,1,0:T(8,128)} %get-tuple-element.11, f32[8,32,16,128]{3,0,2,1:T(8,128)} %bitcast.69, f32[8,27,16,128]{3,0,2,1:T(8,128)} %copy-done.33, ...), kind=kLoop, calls=%fused_computation.162 | loop fusion | flops 22020096 | bytes 40763392 | tf_op jit(solution)/shard_map/mul | solution.py:39
  280.0 0.1 slice.436
  280.2 0.8 copy-done.10
  281.0 0.1 copy-done.14
  281.1 0.1 copy-done.16
  281.4 5.1 broadcast_multiply_fusion.11
  286.5 1.9 collective-permute-start.4
  288.4 0.2 fusion.85
  288.6 4.4 collective-permute-start.5
  293.0 18.1 %collective-permute-done.4 = f32[8,27,16,128]{3,0,2,1:T(8,128)S(1)} collective-permute-done((f32[8,27,16,128]{3,0,2,1:T(8,128)S(1)}, f32[8,27,16,128]{3,0,2,1:T(8,128)S(1)}, u32[]{:S(2)}, u32[]{:S(2)}) %collective-permute-start.4) | collective-permute-done | bytes 1769504 | tf_op jit(solution)/shard_map/ppermute | solution.py:15
  311.1 1.4 collective-permute-done.5
  312.4 1.2 copy-done.32
  313.7 11.8 %add_multiply_fusion.1 = f32[8,32,16,128]{3,0,2,1:T(8,128)} fusion(f32[8,32,16,128]{3,0,2,1:T(8,128)} %get-tuple-element.10, f32[8,27,16,128]{3,0,2,1:T(8,128)} %copy-done.32, f32[8,32,16,128]{3,0,2,1:T(8,128)} %get-tuple-element.40, f32[8,32,16,128]{3,0,2,1:T(8,128)S(1)} %get-tuple-element.9, f32[8,32,16,128]{3,0,2,1:T(8,128)} %get-tuple-element.47, ...), kind=kLoop, calls=%fused_computation.141 | loop fusion | flops 22020096 | bytes 36306944 | tf_op jit(solution)/shard_map/mul | solution.py:78
  325.5 2.5 pad_maximum_fusion.1
  328.0 36.0 %all_to_all.10 = f32[2,8,65536]{2,1,0:T(8,128)} all-to-all(f32[2,8,65536]{2,1,0:T(8,128)S(1)} %pad_maximum_fusion.1), channel_id=1, replica_groups=mesh['brick'=64,'vec'=2] {'vec'}, dimensions={0} | all-to-all | bytes 8388608 | tf_op jit(solution)/shard_map/all_to_all | solution.py:87
  364.0 6.9 fusion
  370.9 151.7 %psum.22 = f32[16,16]{1,0:T(8,128)S(1)} all-reduce(f32[16,16]{1,0:T(8,128)S(1)} %fusion), channel_id=1, replica_groups=mesh['brick'=64,'vec'=2] {'brick'}, use_global_device_ids=true, to_apply=%region_3.6 | all-reduce | flops 256 | bytes 2048 | tf_op jit(solution)/shard_map/psum | solution.py:98
  522.6 7.1 %convolution_subtract_fusion = f32[16,65536]{1,0:T(8,128)S(1)} fusion(f32[16,16]{1,0:T(8,128)S(1)} %psum.22, f32[16,65536]{1,0:T(8,128)} %copy-done.1, f32[2,8,65536]{2,1,0:T(8,128)} %all_to_all.10), kind=kOutput, calls=%fused_computation | convolution fusion | flops 202375168 | bytes 12583936 | tf_op jit(solution)/shard_map/ij,jn->in/dot_general | solution.py:107
  529.7 2.0 copy-done
  531.7 5.6 fusion.132
  537.3 140.5 %psum.23 = f32[16,16]{0,1:T(8,128)S(1)} all-reduce(f32[16,16]{0,1:T(8,128)S(1)} %fusion.132), channel_id=1, replica_groups=mesh['brick'=64,'vec'=2] {'brick'}, use_global_device_ids=true, to_apply=%region_4.7 | all-reduce | flops 256 | bytes 2048 | tf_op jit(solution)/shard_map/psum | solution.py:98
  677.9 1.5 cholesky.55
  679.3 0.6 compare_reduce_fusion
  680.0 1.2 select_bitcast_fusion
  681.2 1.2 custom-call.7
  682.5 5.4 fusion.125
  687.9 0.1 dynamic-slice_multiply_fusion
  688.0 1.7 copy.9
  (69 shorter events, 0.7 us)
Async XLA Ops:
  8.0 58.0 %all-to-all-start = ((f32[2,8,65536]{2,1,0:T(8,128)}), f32[2,8,65536]{2,1,0:T(8,128)}, u32[]{:S(2)}, u32[]{:S(2)}) async-start(f32[2,8,65536]{2,1,0:T(8,128)} %pad_maximum_fusion), calls=%async_computation | async-start | bytes 8388608 | tf_op jit(solution)/shard_map/all_to_all | solution.py:87
  14.4 12.7 %collective-permute-start = (f32[1,27,16,128]{3,2,1,0:T(8,128)}, f32[1,27,16,128]{3,2,1,0:T(8,128)}, u32[]{:S(2)}, u32[]{:S(2)}) collective-permute-start(f32[1,27,16,128]{3,2,1,0:T(8,128)} %slice.322), channel_id=1, source_target_pairs={{2,0},{4,2},{6,4},{8,6},{10,8},{12,10},{14,12},{16,14},{18,16},{20... | collective-permute-start | bytes 663560 | tf_op jit(solution)/shard_map/ppermute | solution.py:15
  20.7 0.7 copy-start.25
  20.7 1.4 copy-start.27
  20.7 4.6 copy-start.29
  22.1 6.4 collective-permute-start.1
  25.4 3.2 copy-start.26
  25.4 3.2 copy-start.28
  25.4 3.2 copy-start.30
  25.4 3.2 copy-start.34
  225.7 138.3 %copy-start.1 = (f32[16,65536]{1,0:T(8,128)}, f32[16,65536]{1,0:T(8,128)S(1)}, u32[]{:S(2)}) copy-start(f32[16,65536]{1,0:T(8,128)S(1)} %fusion.2) | copy-start | bytes 12582916
  225.7 1.1 copy-start.23
  225.7 1.4 copy-start.24
  225.8 3.2 copy-start.4
  229.1 7.4 %copy-start.7 = (f32[32,16,128]{2,1,0:T(8,128)S(1)}, f32[32,16,128]{2,1,0:T(8,128)}, u32[]{:S(2)}) copy-start(f32[32,16,128]{2,1,0:T(8,128)} %get-tuple-element.16) | copy-start | bytes 786436
  229.1 7.4 %copy-start.8 = (f32[32,16,128]{2,1,0:T(8,128)S(1)}, f32[32,16,128]{2,1,0:T(8,128)}, u32[]{:S(2)}) copy-start(f32[32,16,128]{2,1,0:T(8,128)} %get-tuple-element.17) | copy-start | bytes 786436
  229.1 7.4 %copy-start.9 = (f32[32,16,128]{2,1,0:T(8,128)S(1)}, f32[32,16,128]{2,1,0:T(8,128)}, u32[]{:S(2)}) copy-start(f32[32,16,128]{2,1,0:T(8,128)} %get-tuple-element.18) | copy-start | bytes 786436
  229.1 7.4 %copy-start.11 = (f32[32,16,128]{2,1,0:T(8,128)S(1)}, f32[32,16,128]{2,1,0:T(8,128)}, u32[]{:S(2)}) copy-start(f32[32,16,128]{2,1,0:T(8,128)} %get-tuple-element.19) | copy-start | bytes 786436
  229.1 7.4 %copy-start.13 = (f32[32,16,128]{2,1,0:T(8,128)S(1)}, f32[32,16,128]{2,1,0:T(8,128)}, u32[]{:S(2)}) copy-start(f32[32,16,128]{2,1,0:T(8,128)} %get-tuple-element.21) | copy-start | bytes 786436
  229.1 7.4 %copy-start.15 = (f32[32,16,128]{2,1,0:T(8,128)S(1)}, f32[32,16,128]{2,1,0:T(8,128)}, u32[]{:S(2)}) copy-start(f32[32,16,128]{2,1,0:T(8,128)} %get-tuple-element.22) | copy-start | bytes 786436
  229.1 7.4 %copy-start.17 = (f32[32,16,128]{2,1,0:T(8,128)S(1)}, f32[32,16,128]{2,1,0:T(8,128)}, u32[]{:S(2)}) copy-start(f32[32,16,128]{2,1,0:T(8,128)} %get-tuple-element.23) | copy-start | bytes 786436
  229.1 7.4 %copy-start.19 = (f32[32,16,128]{2,1,0:T(8,128)S(1)}, f32[32,16,128]{2,1,0:T(8,128)}, u32[]{:S(2)}) copy-start(f32[32,16,128]{2,1,0:T(8,128)} %get-tuple-element.24) | copy-start | bytes 786436
  229.1 7.4 %copy-start.21 = (f32[32,16,128]{2,1,0:T(8,128)S(1)}, f32[32,16,128]{2,1,0:T(8,128)}, u32[]{:S(2)}) copy-start(f32[32,16,128]{2,1,0:T(8,128)} %get-tuple-element.25) | copy-start | bytes 786436
  229.3 24.1 %collective-permute-start.2 = (f32[8,27,16,128]{3,0,2,1:T(8,128)S(1)}, f32[8,27,16,128]{3,0,2,1:T(8,128)}, u32[]{:S(2)}, u32[]{:S(2)}) collective-permute-start(f32[8,27,16,128]{3,0,2,1:T(8,128)S(1)} %slice.428), channel_id=1, source_target_pairs={{2,0},{4,2},{6,4},{8,6},{10,8},{12,10},{14,12},{16,14},{18,16},{20... | collective-permute-start | bytes 5308424 | tf_op jit(solution)/shard_map/ppermute | solution.py:15
  241.6 1.4 copy-start.3
  241.6 2.1 copy-start.6
  241.6 23.4 %copy-start.2 = (f32[8,32,16,128]{3,0,2,1:T(8,128)}, f32[8,32,16,128]{3,0,2,1:T(8,128)S(1)}, u32[]{:S(2)}) copy-start(f32[8,32,16,128]{3,0,2,1:T(8,128)S(1)} %get-tuple-element.55) | copy-start | bytes 6291460
  243.6 21.4 %collective-permute-start.3 = (f32[8,27,16,128]{3,0,2,1:T(8,128)S(1)}, f32[8,27,16,128]{3,0,2,1:T(8,128)S(1)}, u32[]{:S(2)}, u32[]{:S(2)}) collective-permute-start(f32[8,27,16,128]{3,0,2,1:T(8,128)S(1)} %fusion.82), channel_id=1, source_target_pairs={{0,2},{2,4},{4,6},{6,8},{8,10},{10,12},{12,14},{14,16},{16,18},{18... | collective-permute-start | bytes 5308424 | tf_op jit(solution)/shard_map/ppermute | solution.py:15
  265.0 1.3 copy-start.33
  280.0 1.0 copy-start.10
  280.0 1.0 copy-start.12
  280.0 1.1 copy-start.14
  280.0 1.2 copy-start.16
  280.0 1.2 copy-start.18
  280.0 1.3 copy-start.20
  280.0 1.4 copy-start.22
  286.5 2.1 copy-start.5
  286.5 24.6 %collective-permute-start.4 = (f32[8,27,16,128]{3,0,2,1:T(8,128)S(1)}, f32[8,27,16,128]{3,0,2,1:T(8,128)S(1)}, u32[]{:S(2)}, u32[]{:S(2)}) collective-permute-start(f32[8,27,16,128]{3,0,2,1:T(8,128)S(1)} %slice.436), channel_id=1, source_target_pairs={{2,0},{4,2},{6,4},{8,6},{10,8},{12,10},{14,12},{16,14},{18,16},{20... | collective-permute-start | bytes 5308424 | tf_op jit(solution)/shard_map/ppermute | solution.py:15
  288.6 23.8 %collective-permute-start.5 = (f32[8,27,16,128]{3,0,2,1:T(8,128)S(1)}, f32[8,27,16,128]{3,0,2,1:T(8,128)S(1)}, u32[]{:S(2)}, u32[]{:S(2)}) collective-permute-start(f32[8,27,16,128]{3,0,2,1:T(8,128)S(1)} %fusion.85), channel_id=1, source_target_pairs={{0,2},{2,4},{4,6},{6,8},{8,10},{10,12},{12,14},{14,16},{16,18},{18... | collective-permute-start | bytes 5308424 | tf_op jit(solution)/shard_map/ppermute | solution.py:15
  311.1 1.4 copy-start.31
  312.4 1.2 copy-start.32
  522.5 7.1 %copy-start.35 = (f32[16,16]{1,0:T(8,128)}, f32[16,16]{1,0:T(8,128)S(1)}, u32[]{:S(2)}) copy-start(f32[16,16]{1,0:T(8,128)S(1)} %psum.22) | copy-start | bytes 3076
  529.7 2.0 copy-start
